TPU v7x, 512 devices: a whole 4x8x8 slice. The times are simulated.
512 devices in a mesh: crop: 4 (over x_lo, core), row: 128 (over y, x_hi, z).
Axes of the slice: x: 4 (x_hi: 2, x_lo: 2; x = x_hi * 2 + x_lo), y: 8, z: 8, core: 2. Of those that a mesh axis runs over, the one named last changes fastest.
Arguments:
- pair: bfloat16 [1024, 256, 128], P(('crop', 'row')), parts along dimension 0, may hold values from -6 to 6
- out_grad: bfloat16 [1024, 256, 128], P('crop', 'row'), parts along dimension 0, may hold values from -6 to 6
- w_qkvg: bfloat16 [128, 512], replicated, may hold values from -0.5 to 0.5
- w_out: bfloat16 [128, 128], replicated, may hold values from -0.5 to 0.5
- w_bias: bfloat16 [128, 4], replicated, may hold values from -32 to 32
- gain: float32 [128], replicated, may hold values from 0.1 to 1.9
Outputs:
- d_pair: bfloat16 [1024, 256, 128], P(('crop', 'row')), parts along dimension 0
- d_qkvg: float32 [512, 512], P('crop'), parts along dimension 0
- d_wout: float32 [512, 128], P('crop'), parts along dimension 0
- d_wbias: float32 [512, 4], P('crop'), parts along dimension 0
- d_gain: float32 [512], P('crop'), parts along dimension 0
There are 4 independent parts, one for each index of `crop`. A program takes and returns all parts, laid end to end along the dimension named above; an argument that names none is the same for every part. Nothing has to cross between parts.
All inputs are finite; a program needn't handle non-finite values.
Results may differ from a plain program's by a relative error of at most 0.014.
The roundings to bfloat16 on the way count: a program that leaves them out, or rounds other values in their place, can miss the bound.
Values may be sent and summed in bfloat16 or wider, within the bound.
No kernel may reach another device: no remote copies, remote signals or barrier semaphores. Data moves between devices by JAX's collectives and lax.ppermute only.
A program may use at most 64 MiB of HBM per device.

v0:
```python
import jax
import jax.numpy as jnp
from jax import lax
from jax.sharding import Mesh
from jax.sharding import PartitionSpec as P

DH = 32
ROW = ("row_0", "row_1", "row_2")
CROP_ROW = ("crop", "row_0", "row_1", "row_2")


EPSILON = 1e-05


def sent_to_all(shard, axis):
    copies = jnp.broadcast_to(shard, (lax.axis_size(axis), *shard.shape))
    return lax.all_to_all(copies, axis, split_axis=0, concat_axis=0, tiled=True)


def joined_along(blocks, dim):
    lengths = list(blocks.shape[1:])
    lengths[dim] *= blocks.shape[0]
    return jnp.moveaxis(blocks, 0, dim).reshape(lengths)


def gathered_by_axis(shard, axes, dim):
    far, near = axes
    initial = sent_to_all(shard, far)
    blocks = jnp.swapaxes(sent_to_all(initial, near), 0, 1)
    return joined_along(blocks.reshape(-1, *shard.shape), dim)


def cut_along(shard, dim, count):
    before, after = (shard.shape[:dim], shard.shape[dim + 1 :])
    return jnp.moveaxis(shard.reshape(*before, count, -1, *after), dim, 0)


def sum_at_owner(shard, axis, dim):
    count = lax.axis_size(axis)
    blocks = lax.all_to_all(cut_along(shard, dim, count), axis, 0, 0, tiled=True)
    return jnp.sum(blocks, axis=0)


def sum_in_two_steps(shard, axes, dim):
    far, near = axes
    blocks = cut_along(shard, dim, lax.axis_size(far))
    nearer = sum_at_owner(blocks, near, dim + 1)
    arrived = lax.all_to_all(nearer, far, split_axis=0, concat_axis=0, tiled=True)
    return arrived.sum(axis=0)


def filled_up(lines, count):
    spare = -lines.shape[0] % count
    if not spare:
        return lines
    return jnp.concatenate([lines, jnp.zeros((spare, *lines.shape[1:]), lines.dtype)])


def nested_sum(shard, axes):
    own = sum_in_two_steps(
        filled_up(shard, lax.axis_size(axes[0]) * lax.axis_size(axes[1])), axes, 0
    )
    whole = gathered_by_axis(own, axes, 0)
    return whole[: len(shard)].reshape(shard.shape)


def packed_total(arrays, axis):
    line, at, gathered = (jnp.concatenate([a.reshape(-1) for a in arrays]), 0, [])
    subtotal = nested_sum(line, axis)
    for a in arrays:
        gathered.append(subtotal[at : at + a.size].reshape(a.shape))
        at += a.size
    return tuple(gathered)


def normalize(pair, gain):
    values = pair.astype(jnp.float32)
    center = jnp.mean(values, axis=-1, keepdims=True)
    spread = jnp.mean(jnp.square(values - center), axis=-1, keepdims=True)
    inv_std = lax.rsqrt(spread + EPSILON)
    normed = (values - center) * inv_std
    return ((normed * gain).astype(jnp.bfloat16), normed, inv_std)


def column_grad(tokens, grads, w_qkvg, w_out, bias, scale):
    width = w_out.shape[0]
    heads = bias.shape[0]
    size = width // heads
    count = tokens.shape[0]
    proj = jnp.dot(tokens, w_qkvg, preferred_element_type=jnp.float32)
    queries = proj[:, :width].astype(jnp.bfloat16).reshape(count, heads, size)
    keys = proj[:, width : 2 * width].astype(jnp.bfloat16).reshape(count, heads, size)
    values = proj[:, 2 * width : 3 * width].astype(jnp.bfloat16).reshape(count, heads, size)
    gate = jax.nn.sigmoid(proj[:, 3 * width :]).reshape(count, heads, size)
    scores = jnp.einsum("khd,ihd->hki", keys, queries, preferred_element_type=jnp.float32) * scale
    scores = scores + bias.astype(jnp.float32)
    probs = jax.nn.softmax(scores, axis=1)
    probs_b = probs.astype(jnp.bfloat16)
    attended = jnp.einsum("hki,khd->ihd", probs_b, values, preferred_element_type=jnp.float32)
    mixed = (gate * attended).astype(jnp.bfloat16).reshape(count, width)
    d_mixed = lax.dot_general(
        grads, w_out, (((1,), (1,)), ((), ())), preferred_element_type=jnp.float32
    ).reshape(count, heads, size)
    part_wout = lax.dot_general(
        mixed, grads, (((0,), (0,)), ((), ())), preferred_element_type=jnp.float32
    )
    d_gate = d_mixed * attended * gate * (1.0 - gate)
    d_att = (d_mixed * gate).astype(jnp.bfloat16)
    d_values = jnp.einsum("hki,ihd->khd", probs_b, d_att, preferred_element_type=jnp.float32)
    d_probs = jnp.einsum("ihd,khd->hki", d_att, values, preferred_element_type=jnp.float32)
    delta = jnp.sum(d_att.astype(jnp.float32) * attended, axis=-1)
    d_scores = (probs * (d_probs - delta.T[:, None, :])).astype(jnp.bfloat16)
    d_queries = (
        jnp.einsum("hki,khd->ihd", d_scores, keys, preferred_element_type=jnp.float32) * scale
    )
    d_keys = (
        jnp.einsum("hki,ihd->khd", d_scores, queries, preferred_element_type=jnp.float32) * scale
    )
    d_proj = jnp.concatenate(
        [
            d_queries.reshape(count, width),
            d_keys.reshape(count, width),
            d_values.reshape(count, width),
            d_gate.reshape(count, width),
        ],
        axis=1,
    ).astype(jnp.bfloat16)
    part_qkvg = lax.dot_general(
        tokens, d_proj, (((0,), (0,)), ((), ())), preferred_element_type=jnp.float32
    )
    d_tokens = lax.dot_general(
        d_proj, w_qkvg, (((1,), (1,)), ((), ())), preferred_element_type=jnp.float32
    ).astype(jnp.bfloat16)
    return (d_tokens, d_scores, part_qkvg, part_wout, queries, keys, values, d_att, delta)


def per_device(pair, out_grad, w_qkvg, w_out, w_bias, gain):
    normed_b, normed, inv_std = normalize(pair, gain)
    width = w_out.shape[0]
    heads = w_bias.shape[1]
    scale = DH ** (-0.5)
    columns = lax.all_to_all(normed_b, ROW, split_axis=1, concat_axis=0, tiled=True)
    wide_bias = w_bias.astype(jnp.float32)
    local_bias = jnp.einsum(
        "abc,ch->hab", normed_b, w_bias, preferred_element_type=jnp.float32
    ).astype(jnp.bfloat16)
    bias = gathered_by_axis(local_bias, ("row_0", ("row_1", "row_2")), 1)
    length = bias.shape[1]
    inv_count = 1.0 / length
    inputs = (jnp.swapaxes(columns, 0, 1), jnp.swapaxes(out_grad, 0, 1))

    def step(carry, pieces):
        d_bias, d_qkvg, d_wout = carry
        outs = column_grad(pieces[0], pieces[1], w_qkvg, w_out, bias, scale)
        return ((d_bias + outs[1].astype(jnp.float32), d_qkvg + outs[2], d_wout + outs[3]), outs[0])

    start = (
        jnp.zeros((heads, length, length), jnp.float32),
        jnp.zeros((width, 4 * width), jnp.float32),
        jnp.zeros((width, width), jnp.float32),
    )
    (d_bias, d_qkvg, d_wout), d_cols = lax.scan(step, start, inputs)
    d_att_cols = jnp.swapaxes(d_cols, 0, 1)
    owned = sum_in_two_steps(d_bias, ("row_0", ("row_1", "row_2")), 1)
    d_att_x = lax.all_to_all(d_att_cols, ROW, split_axis=0, concat_axis=1, tiled=True)
    d_bias_x = jnp.einsum("hab,ch->abc", owned, wide_bias, precision=lax.Precision.HIGHEST).astype(
        jnp.bfloat16
    )
    d_wbias = jnp.einsum(
        "abc,hab->ch", normed_b.astype(jnp.float32), owned, precision=lax.Precision.HIGHEST
    )
    d_xn = d_att_x.astype(jnp.float32) + d_bias_x.astype(jnp.float32)
    local_gain = jnp.sum(d_xn * normed, axis=(0, 1))
    scaled = d_xn * gain
    d_pair = (
        inv_std
        * (
            scaled
            - jnp.mean(scaled, axis=-1, keepdims=True)
            - normed * jnp.mean(scaled * normed, axis=-1, keepdims=True)
        )
    ).astype(jnp.bfloat16)
    total_qkvg, total_wout, total_wbias, total_gain = packed_total(
        (d_qkvg, d_wout, d_wbias, local_gain), ("row_0", ("row_1", "row_2"))
    )
    return (
        d_pair,
        total_qkvg * inv_count,
        total_wout * inv_count,
        total_wbias * inv_count,
        total_gain * inv_count,
    )


def solution(mesh):
    split = Mesh(
        mesh.devices.reshape(mesh.shape["crop"], 8, 2, 8), ("crop", "row_0", "row_1", "row_2")
    )
    placed = (P(CROP_ROW, None, None), P("crop", ROW, None), P(), P(), P(), P())
    return jax.shard_map(
        per_device,
        mesh=split,
        in_specs=placed,
        out_specs=(
            P(CROP_ROW, None, None),
            P("crop", None),
            P("crop", None),
            P("crop", None),
            P("crop"),
        ),
        check_vma=False,
    )
```

profile of v0, /device:TPU:2, one launch (start us, length us, event | category | flops | bytes accessed | tf_op | source)
XLA Modules:
  0.0 214.8 jit_solution(15475856017583670832)
XLA Ops:
  0.6 1.0 copy.140
  1.8 0.7 fusion.41
  2.7 0.6 broadcast_in_dim.41
  3.3 7.1 %all-to-all-start.1 = ((bf16[8,4,2,256]{3,2,1,0:T(2,128)(2,1)}), bf16[8,4,2,256]{3,2,1,0:T(2,128)(2,1)S(1)}, u32[]{:S(2)}, u32[]{:S(2)}) async-start(bf16[8,4,2,256]{3,2,1,0:T(2,128)(2,1)} %broadcast_in_dim.41), calls=%async_computation.1 | async-start | bytes 65536 | tf_op jit(solution)/shard_map/all_to_all | solution.py:17
  10.4 0.8 copy.141
  11.2 7.2 %all-to-all-done.1 = bf16[8,4,2,256]{3,2,1,0:T(2,128)(2,1)S(1)} async-done(((bf16[8,4,2,256]{3,2,1,0:T(2,128)(2,1)}), bf16[8,4,2,256]{3,2,1,0:T(2,128)(2,1)S(1)}, u32[]{:S(2)}, u32[]{:S(2)}) %all-to-all-start.1) | async-done | bytes 32800 | tf_op jit(solution)/shard_map/all_to_all | solution.py:17
  18.5 14.1 %all-to-all-start = ((bf16[2,256,128]{2,0,1:T(2,128)(2,1)}), bf16[2,256,128]{2,0,1:T(2,128)(2,1)S(1)}, u32[]{:S(2)}, u32[]{:S(2)}) async-start(bf16[2,256,128]{2,0,1:T(2,128)(2,1)} %copy.141), calls=%async_computation | async-start | bytes 262144 | tf_op jit(solution)/shard_map/all_to_all | solution.py:142
  32.6 14.6 %all-to-all-done = bf16[2,256,128]{2,0,1:T(2,128)(2,1)S(1)} async-done(((bf16[2,256,128]{2,0,1:T(2,128)(2,1)}), bf16[2,256,128]{2,0,1:T(2,128)(2,1)S(1)}, u32[]{:S(2)}, u32[]{:S(2)}) %all-to-all-start) | async-done | bytes 131104 | tf_op jit(solution)/shard_map/all_to_all | solution.py:142
  47.2 1.2 broadcast_in_dim.42
  48.4 3.6 %all-to-all-start.2 = ((bf16[16,8,4,2,256]{4,3,1,2,0:T(2,128)(2,1)}), bf16[16,8,4,2,256]{4,3,1,2,0:T(2,128)(2,1)S(1)}, u32[]{:S(2)}, u32[]{:S(2)}) async-start(bf16[16,8,4,2,256]{4,3,1,2,0:T(2,128)(2,1)} %broadcast_in_dim.42), calls=%async_computation.2 | async-start | bytes 1048576 | tf_op jit(solution)/shard_map/all_to_all | solution.py:17
  52.0 0.9 copy.187
  53.1 13.6 %all-to-all-done.2 = bf16[16,8,4,2,256]{4,3,1,2,0:T(2,128)(2,1)S(1)} async-done(((bf16[16,8,4,2,256]{4,3,1,2,0:T(2,128)(2,1)}), bf16[16,8,4,2,256]{4,3,1,2,0:T(2,128)(2,1)S(1)}, u32[]{:S(2)}, u32[]{:S(2)}) %all-to-all-start.2) | async-done | bytes 524320 | tf_op jit(solution)/shard_map/all_to_all | solution.py:17
  66.7 0.3 copy.147
  67.0 0.4 copy.148
  67.4 0.9 copy.150
  68.2 14.5 %while.17 = (s32[]{:T(128)}, f32[4,256,256]{2,1,0:T(8,128)S(1)}, f32[128,512]{1,0:T(8,128)S(1)}, f32[128,128]{1,0:T(8,128)S(1)}, bf16[2,256,128]{2,1,0:T(8,128)(...) while((s32[]{:T(128)}, f32[4,256,256]{2,1,0:T(8,128)S(1)}, ...), condition=%wide.region_6.7_spmd.clone, body=%wide.region_2.6_spmd.clone.sunk | while | flops 224853248 | bytes 14733497 | solution.py:162
  68.2 0.9 fusion.120
  69.2 1.1 fusion.121
  70.8 1.6 fusion.124
  72.5 0.2 multiply_reduce_fusion.3
  72.8 0.2 convolution_convert_fusion.5
  73.2 0.6 select_add_fusion.2
  74.0 0.3 fusion.126
  74.3 0.9 fusion.128
  75.2 0.3 convolution_add_fusion.4
  75.5 1.0 fusion.120
  76.4 1.1 fusion.121
  78.1 1.6 fusion.124
  79.8 0.2 multiply_reduce_fusion.3
  80.0 0.2 convolution_convert_fusion.5
  80.5 0.6 select_add_fusion.2
  81.3 0.3 fusion.126
  81.6 0.9 fusion.128
  82.5 0.3 convolution_add_fusion.4
  82.7 0.6 copy.153
  83.4 1.5 copy.154
  84.9 4.7 %all-to-all-start.4 = ((f32[16,8,4,2,256]{4,3,1,2,0:T(2,128)}), f32[16,8,4,2,256]{4,3,1,2,0:T(2,128)S(1)}, u32[]{:S(2)}, u32[]{:S(2)}) async-start(f32[16,8,4,2,256]{4,3,1,2,0:T(2,128)} %copy.154), calls=%async_computation.4 | async-start | bytes 2097152 | tf_op jit(solution)/shard_map/all_to_all | solution.py:40
  89.6 1.7 copy.186
  91.3 25.2 %all-to-all-done.4 = f32[16,8,4,2,256]{4,3,1,2,0:T(2,128)S(1)} async-done(((f32[16,8,4,2,256]{4,3,1,2,0:T(2,128)}), f32[16,8,4,2,256]{4,3,1,2,0:T(2,128)S(1)}, u32[]{:S(2)}, u32[]{:S(2)}) %all-to-all-start.4) | async-done | bytes 1048608 | tf_op jit(solution)/shard_map/all_to_all | solution.py:40
  116.5 7.4 %all-to-all-start.3 = ((bf16[256,2,128]{2,1,0:T(2,128)(2,1)}), bf16[256,2,128]{2,1,0:T(2,128)(2,1)S(1)}, u32[]{:S(2)}, u32[]{:S(2)}) async-start(bf16[256,2,128]{2,1,0:T(2,128)(2,1)} %bitcast.99), calls=%async_computation.3 | async-start | bytes 262144 | tf_op jit(solution)/shard_map/all_to_all | solution.py:165
  123.9 0.5 reduce_sum.101
  124.4 0.6 copy.156
  125.0 13.5 %all-to-all-done.3 = bf16[256,2,128]{2,1,0:T(2,128)(2,1)S(1)} async-done(((bf16[256,2,128]{2,1,0:T(2,128)(2,1)}), bf16[256,2,128]{2,1,0:T(2,128)(2,1)S(1)}, u32[]{:S(2)}, u32[]{:S(2)}) %all-to-all-start.3) | async-done | bytes 131104 | tf_op jit(solution)/shard_map/all_to_all | solution.py:165
  138.5 3.5 %all-to-all-start.5 = ((f32[8,4,2,256]{3,2,1,0:T(2,128)}), f32[8,4,2,256]{3,2,1,0:T(2,128)S(1)}, u32[]{:S(2)}, u32[]{:S(2)}) async-start(f32[8,4,2,256]{3,2,1,0:T(2,128)} %copy.156), calls=%async_computation.5 | async-start | bytes 131072 | tf_op jit(solution)/shard_map/all_to_all | solution.py:48
  142.4 7.8 %all-to-all-done.5 = f32[8,4,2,256]{3,2,1,0:T(2,128)S(1)} async-done(((f32[8,4,2,256]{3,2,1,0:T(2,128)}), f32[8,4,2,256]{3,2,1,0:T(2,128)S(1)}, u32[]{:S(2)}, u32[]{:S(2)}) %all-to-all-start.5) | async-done | bytes 65568 | tf_op jit(solution)/shard_map/all_to_all | solution.py:48
  150.2 0.2 convolution_bitcast_fusion.1
  150.6 1.1 fusion.46
  151.7 0.4 reshape_reshape.6
  152.1 0.2 copy.163
  152.3 14.4 %all_to_all.75 = f32[16,8,645]{2,1,0:T(8,128)S(1)} all-to-all(f32[16,8,645]{2,1,0:T(8,128)S(1)} %copy.163), channel_id=1, replica_groups=mesh['crop'=4,'row_0'=8,'row_1'=2,'row_2'=8] {'row_1','row_2'}, dimensions={0} | all-to-all | bytes 660480 | tf_op jit(solution)/shard_map/all_to_all | solution.py:40
  166.8 10.3 %all_to_all.76 = f32[8,1,645]{2,1,0:T(1,128)S(1)} all-to-all(f32[8,1,645]{2,1,0:T(1,128)S(1)} %all_to_all.60), channel_id=1, replica_groups=mesh['crop'=4,'row_0'=8,'row_1'=2,'row_2'=8] {'row_0'}, dimensions={0} | all-to-all | bytes 41280 | tf_op jit(solution)/shard_map/all_to_all | solution.py:48
  177.1 10.3 %all_to_all.77 = f32[8,1,645]{2,1,0:T(1,128)S(1)} all-to-all(f32[8,1,645]{2,1,0:T(1,128)S(1)} %broadcast_in_dim.43), channel_id=1, replica_groups=mesh['crop'=4,'row_0'=8,'row_1'=2,'row_2'=8] {'row_0'}, dimensions={0} | all-to-all | bytes 41280 | tf_op jit(solution)/shard_map/all_to_all | solution.py:17
  187.4 0.8 broadcast_in_dim.44
  188.2 4.3 %all-to-all-start.9 = ((f32[16,8,645]{2,1,0:T(8,128)}), f32[16,8,645]{2,1,0:T(8,128)S(1)}, u32[]{:S(2)}, u32[]{:S(2)}) async-start(f32[16,8,645]{2,1,0:T(8,128)} %broadcast_in_dim.44), calls=%async_computation.9 | async-start | bytes 786432 | tf_op jit(solution)/shard_map/all_to_all | solution.py:17
  192.7 0.8 copy.167
  193.4 10.9 %all-to-all-done.9 = f32[16,8,645]{2,1,0:T(8,128)S(1)} async-done(((f32[16,8,645]{2,1,0:T(8,128)}), f32[16,8,645]{2,1,0:T(8,128)S(1)}, u32[]{:S(2)}, u32[]{:S(2)}) %all-to-all-start.9) | async-done | bytes 330272 | tf_op jit(solution)/shard_map/all_to_all | solution.py:17
  204.5 0.3 reshape_reshape.7
  204.8 0.5 slice_multiply_fusion.3
  205.4 0.3 slice.34
  205.7 6.2 %slice.36 = f32[20640,4]{1,0:T(8,128)} reshape(f32[8,16,645]{2,1,0:T(8,128)S(1)} %copy.164) | data formatting | bytes 660480 | tf_op jit(solution)/shard_map/slice | solution.py:71
  211.9 0.7 mul.117
  212.6 0.6 slice_multiply_fusion.2
  213.3 0.8 slice_multiply_fusion.1
  214.1 0.7 copy.168
  (54 shorter events, 3.2 us)
Async XLA Ops:
  0.6 1.9 copy-start
  3.3 15.1 %all-to-all-start.1 = ((bf16[8,4,2,256]{3,2,1,0:T(2,128)(2,1)}), bf16[8,4,2,256]{3,2,1,0:T(2,128)(2,1)S(1)}, u32[]{:S(2)}, u32[]{:S(2)}) async-start(bf16[8,4,2,256]{3,2,1,0:T(2,128)(2,1)} %broadcast_in_dim.41), calls=%async_computation.1 | async-start | bytes 65536 | tf_op jit(solution)/shard_map/all_to_all | solution.py:17
  18.5 28.7 %all-to-all-start = ((bf16[2,256,128]{2,0,1:T(2,128)(2,1)}), bf16[2,256,128]{2,0,1:T(2,128)(2,1)S(1)}, u32[]{:S(2)}, u32[]{:S(2)}) async-start(bf16[2,256,128]{2,0,1:T(2,128)(2,1)} %copy.141), calls=%async_computation | async-start | bytes 262144 | tf_op jit(solution)/shard_map/all_to_all | solution.py:142
  48.4 18.3 %all-to-all-start.2 = ((bf16[16,8,4,2,256]{4,3,1,2,0:T(2,128)(2,1)}), bf16[16,8,4,2,256]{4,3,1,2,0:T(2,128)(2,1)S(1)}, u32[]{:S(2)}, u32[]{:S(2)}) async-start(bf16[16,8,4,2,256]{4,3,1,2,0:T(2,128)(2,1)} %broadcast_in_dim.42), calls=%async_computation.2 | async-start | bytes 1048576 | tf_op jit(solution)/shard_map/all_to_all | solution.py:17
  68.2 6.0 %copy-start.1 = (bf16[128,512]{1,0:T(8,128)(2,1)S(1)}, bf16[128,512]{1,0:T(8,128)(2,1)}, u32[]{:S(2)}) copy-start(bf16[128,512]{1,0:T(8,128)(2,1)} %get-tuple-element.308) | copy-start | bytes 393220 | tf_op jit(solution)/shard_map/while
  75.5 6.1 %copy-start.1 = (bf16[128,512]{1,0:T(8,128)(2,1)S(1)}, bf16[128,512]{1,0:T(8,128)(2,1)}, u32[]{:S(2)}) copy-start(bf16[128,512]{1,0:T(8,128)(2,1)} %get-tuple-element.308) | copy-start | bytes 393220 | tf_op jit(solution)/shard_map/while
  82.7 109.8 %copy-start.2 = (f32[128]{0:T(128)S(1)}, f32[128]{0:T(128)}, u32[]{:S(2)}) copy-start(f32[128]{0:T(128)} %param.13) | copy-start | bytes 1540
  84.9 31.6 %all-to-all-start.4 = ((f32[16,8,4,2,256]{4,3,1,2,0:T(2,128)}), f32[16,8,4,2,256]{4,3,1,2,0:T(2,128)S(1)}, u32[]{:S(2)}, u32[]{:S(2)}) async-start(f32[16,8,4,2,256]{4,3,1,2,0:T(2,128)} %copy.154), calls=%async_computation.4 | async-start | bytes 2097152 | tf_op jit(solution)/shard_map/all_to_all | solution.py:40
  116.5 22.0 %all-to-all-start.3 = ((bf16[256,2,128]{2,1,0:T(2,128)(2,1)}), bf16[256,2,128]{2,1,0:T(2,128)(2,1)S(1)}, u32[]{:S(2)}, u32[]{:S(2)}) async-start(bf16[256,2,128]{2,1,0:T(2,128)(2,1)} %bitcast.99), calls=%async_computation.3 | async-start | bytes 262144 | tf_op jit(solution)/shard_map/all_to_all | solution.py:165
  138.5 11.7 %all-to-all-start.5 = ((f32[8,4,2,256]{3,2,1,0:T(2,128)}), f32[8,4,2,256]{3,2,1,0:T(2,128)S(1)}, u32[]{:S(2)}, u32[]{:S(2)}) async-start(f32[8,4,2,256]{3,2,1,0:T(2,128)} %copy.156), calls=%async_computation.5 | async-start | bytes 131072 | tf_op jit(solution)/shard_map/all_to_all | solution.py:48
  188.2 16.2 %all-to-all-start.9 = ((f32[16,8,645]{2,1,0:T(8,128)}), f32[16,8,645]{2,1,0:T(8,128)S(1)}, u32[]{:S(2)}, u32[]{:S(2)}) async-start(f32[16,8,645]{2,1,0:T(8,128)} %broadcast_in_dim.44), calls=%async_computation.9 | async-start | bytes 786432 | tf_op jit(solution)/shard_map/all_to_all | solution.py:17
where the time goes:
time: 216 us; the launch traced here: 215 us
  waiting for transfers between devices  92.8 us (43%)
  starting transfers between devices  44.7 us (21%)
  blocking collectives  35 us (16%)
  local copies, waits for them, and re-layouts  22.6 us (10%)
  matrix products  14.5 us (7%)
  other arithmetic  3.91 us (2%)
    all_to_all x3, waiting for transfers between devices, sent_to_all(): return lax.all_to_all(copies, axis, split_axis=0, concat_axis=0, tiled=True)  31.7 us
    all_to_all x1, waiting for transfers between devices, sum_at_owner(): lax.all_to_all(cut_along(shard, dim, count), axis, 0, 0, tiled=True)  25.2 us
    all_to_all x3, starting transfers between devices, sent_to_all(): return lax.all_to_all(copies, axis, split_axis=0, concat_axis=0, tiled=True)  15 us
    all_to_all x1, waiting for transfers between devices, per_device(): lax.all_to_all(normed_b, ROW, split_axis=1, concat_axis=0, tiled=True)  14.6 us
    all_to_all x1, blocking collectives, sum_at_owner(): lax.all_to_all(cut_along(shard, dim, count), axis, 0, 0, tiled=True)  14.4 us
    all_to_all x1, starting transfers between devices, per_device(): lax.all_to_all(normed_b, ROW, split_axis=1, concat_axis=0, tiled=True)  14.1 us
    all_to_all x1, waiting for transfers between devices, per_device(): lax.all_to_all(d_att_cols, ROW, split_axis=0, concat_axis=1, tiled=True)  13.5 us
    all_to_all x1, blocking collectives, sent_to_all(): return lax.all_to_all(copies, axis, split_axis=0, concat_axis=0, tiled=True)  10.3 us
  transfers between devices with their start and end apart: 7, of which 7 were waited for; matrix products, arithmetic and copies ran while one was open for 3% of the time, Pallas kernels for 0%

commit v1 on v0

v1 whole, which is shorter than its diff:
```python
import jax
import jax.numpy as jnp
from jax import lax
from jax.experimental import pallas as pl
from jax.experimental.pallas import tpu as pltpu
from jax.sharding import Mesh
from jax.sharding import PartitionSpec as P

DH = 32
H = 4
C = 128
N = 256
DEV = 128
SCALE = DH ** (-0.5)
ROW = ("row_0", "row_1", "row_2")
CROP_ROW = ("crop", "row_0", "row_1", "row_2")
EPSILON = 1e-05
F32 = jnp.float32
BF16 = jnp.bfloat16


def dot(a, b, ca=1, cb=0):
    return lax.dot_general(a, b, (((ca,), (cb,)), ((), ())), preferred_element_type=F32)


def normalize(pair, gain):
    values = pair.astype(F32)
    center = jnp.mean(values, axis=-1, keepdims=True)
    spread = jnp.mean(jnp.square(values - center), axis=-1, keepdims=True)
    inv_std = lax.rsqrt(spread + EPSILON)
    normed = (values - center) * inv_std
    return ((normed * gain).astype(BF16), normed, inv_std)


def attention_kernel(cols_ref, grad_ref, w_ref, wt_ref, wout_ref, out_ref, dbias_ref):
    lane = lax.broadcasted_iota(jnp.int32, (N, C), 1) // DH
    zero = jnp.zeros((N, C), BF16)
    d_w = d_wout = None
    for c in range(2):
        tokens = jnp.concatenate([cols_ref[16 + c], cols_ref[18 + c]], axis=0)
        grads = grad_ref[c]
        proj = dot(tokens, w_ref[:, : 3 * C]).astype(BF16)
        q, k, v = proj[:, :C], proj[:, C : 2 * C], proj[:, 2 * C :]
        proj_t = dot(wt_ref[...], tokens, 1, 1)
        q_t = proj_t[:C].astype(BF16)
        k_t = proj_t[C : 2 * C].astype(BF16)
        v_t = proj_t[2 * C : 3 * C].astype(BF16)
        gate_t = jax.nn.sigmoid(proj_t[3 * C :])
        d_mixed_t = dot(wout_ref[...], grads, 1, 1)
        d_att_t = (d_mixed_t * gate_t).astype(BF16)
        d_att = d_att_t.T
        att_t, dq_t = [], []
        d_k = d_v = None
        for h in range(H):
            own = lane == h
            rows = slice(h * DH, (h + 1) * DH)
            bias = jnp.concatenate(
                [
                    jnp.concatenate([cols_ref[4 * h + 2 * r], cols_ref[4 * h + 2 * r + 1]], axis=1)
                    for r in range(2)
                ],
                axis=0,
            ).astype(F32)
            s = dot(jnp.where(own, k, zero), q_t) * SCALE + bias
            e = jnp.exp(s - jnp.max(s, axis=0, keepdims=True))
            probs = e * (1.0 / jnp.sum(e, axis=0, keepdims=True))
            probs_b = probs.astype(BF16)
            att_h = dot(v_t[rows], probs_b)
            delta = jnp.sum(d_att_t[rows].astype(F32) * att_h, axis=0, keepdims=True)
            d_probs = dot(jnp.where(own, v, zero), d_att_t)
            d_s = (probs * (d_probs - delta)).astype(BF16)
            att_t.append(att_h)
            dq_t.append(dot(k_t[rows], d_s))
            dk_h = dot(d_s, jnp.where(own, q, zero))
            dv_h = dot(probs_b, jnp.where(own, d_att, zero))
            d_k = dk_h if d_k is None else d_k + dk_h
            d_v = dv_h if d_v is None else d_v + dv_h
            if c == 0:
                dbias_ref[h] = d_s
            else:
                total = (dbias_ref[h].astype(F32) + d_s.astype(F32)).astype(BF16)
                for r in range(2):
                    for half in range(2):
                        out_ref[4 * h + 2 * r + half] = total[
                            r * 128 : (r + 1) * 128, half * 128 : (half + 1) * 128
                        ]
        att_t = jnp.concatenate(att_t, axis=0)
        mixed_t = (gate_t * att_t).astype(BF16)
        d_gate_t = (d_mixed_t * att_t * gate_t * (1.0 - gate_t)).astype(BF16)
        d_q_t = (jnp.concatenate(dq_t, axis=0) * SCALE).astype(BF16)
        d_proj = jnp.concatenate(
            [d_q_t.T, (d_k * SCALE).astype(BF16), d_v.astype(BF16), d_gate_t.T], axis=1
        )
        part_wout = dot(mixed_t, grads)
        part_w = dot(tokens, d_proj, 0, 0)
        d_w = part_w if d_w is None else d_w + part_w
        d_wout = part_wout if d_wout is None else d_wout + part_wout
        d_tokens = dot(d_proj, wt_ref[...]).astype(BF16)
        out_ref[16 + c] = d_tokens[:128]
        out_ref[18 + c] = d_tokens[128:]
    for block in range(4):
        out_ref[20 + block] = d_w[:, block * C : (block + 1) * C].astype(BF16)
    out_ref[24] = d_wout.astype(BF16)


def attention(cols, grads, w, w_t, w_out):
    return pl.pallas_call(
        attention_kernel,
        out_shape=jax.ShapeDtypeStruct((25, DEV, C), BF16),
        scratch_shapes=[pltpu.VMEM((H, N, N), BF16)],
        cost_estimate=pl.CostEstimate(
            flops=900_000_000, bytes_accessed=3_000_000, transcendentals=600_000
        ),
    )(cols, grads, w, w_t, w_out)


def exchanged(blocks):
    return lax.all_to_all(blocks, ROW, split_axis=0, concat_axis=0, tiled=True)


def per_device(pair, out_grad, w_qkvg, w_out, w_bias, gain):
    pair = pair.reshape(2, 128, 2, C).transpose(0, 2, 1, 3)
    xn, normed, inv_std = normalize(pair, gain)
    bias = jnp.einsum("rcpd,dh->hrcp", xn, w_bias, preferred_element_type=F32).astype(BF16)
    sent = jnp.concatenate(
        [
            jnp.broadcast_to(bias.reshape(1, 16, 128), (DEV, 16, 128)),
            xn.reshape(4, 128, C).transpose(1, 0, 2),
        ],
        axis=1,
    )
    cols = exchanged(sent).transpose(1, 0, 2)
    grads = out_grad.reshape(128, 2, 2, C).transpose(2, 1, 0, 3).reshape(2, N, C)
    planes = attention(cols, grads, w_qkvg, w_qkvg.T, w_out)
    back = exchanged(planes.transpose(1, 0, 2))
    summed = jnp.sum(
        jnp.concatenate([back[:, :16], back[:, 20:]], axis=1).astype(F32), axis=0
    )
    d_bias = summed[:16].reshape(H, 2, 2, 128)
    d_att_x = back[:, 16:20].transpose(1, 0, 2).reshape(2, 2, 128, C)
    d_bias_x = jnp.einsum(
        "hrcp,dh->rcpd", d_bias, w_bias.astype(F32), precision=lax.Precision.HIGHEST
    ).astype(BF16)
    d_wbias = jnp.einsum(
        "rcpd,hrcp->hd", xn.astype(F32), d_bias, precision=lax.Precision.HIGHEST
    )
    d_xn = d_att_x.astype(F32) + d_bias_x.astype(F32)
    d_gain = jnp.sum(d_xn * normed, axis=(0, 1, 2))
    scaled = d_xn * gain
    d_pair = (
        inv_std
        * (
            scaled
            - jnp.mean(scaled, axis=-1, keepdims=True)
            - normed * jnp.mean(scaled * normed, axis=-1, keepdims=True)
        )
    ).astype(BF16)
    d_pair = d_pair.transpose(0, 2, 1, 3).reshape(2, N, C)
    own = jnp.concatenate([summed[16:], d_wbias, d_gain[None]], axis=0).astype(BF16)
    last = exchanged(jnp.broadcast_to(own[None], (DEV, 10, C))).astype(F32) * (1.0 / N)
    small = jnp.sum(last[:, 5:], axis=0)
    return (
        d_pair,
        last[:, :4].reshape(C, 4 * C),
        last[:, 4],
        small[:4].T,
        small[4],
    )


def solution(mesh):
    split = Mesh(
        mesh.devices.reshape(mesh.shape["crop"], 8, 2, 8), ("crop", "row_0", "row_1", "row_2")
    )
    placed = (P(CROP_ROW, None, None), P("crop", ROW, None), P(), P(), P(), P())
    return jax.shard_map(
        per_device,
        mesh=split,
        in_specs=placed,
        out_specs=(
            P(CROP_ROW, None, None),
            P("crop", None),
            P("crop", None),
            P("crop", None),
            P("crop"),
        ),
        check_vma=False,
    )
```

time: 216 us -> 133 us (0.62)
  the two profiles are of different devices: /device:TPU:2 before, /device:TPU:8 now
where the time goes in v1:
time: 133 us
  waiting for transfers between devices  45.5 us (34%)
  blocking collectives  38 us (29%)
  starting transfers between devices  26.6 us (20%)
  local copies, waits for them, and re-layouts  9.4 us (7%)
  Pallas kernels  7.68 us (6%)
  other arithmetic  4.12 us (3%)
    all_to_all x2, waiting for transfers between devices, exchanged(): return lax.all_to_all(blocks, ROW, split_axis=0, concat_axis=0, tiled=True)  45.5 us
    all_to_all x1, blocking collectives, exchanged(): return lax.all_to_all(blocks, ROW, split_axis=0, concat_axis=0, tiled=True)  38 us
    all_to_all x2, starting transfers between devices, exchanged(): return lax.all_to_all(blocks, ROW, split_axis=0, concat_axis=0, tiled=True)  26.6 us
    pallas_call x1, Pallas kernels, attention(): pl.pallas_call(attention_kernel, out_shape=jax.ShapeDtypeStruct((25, DEV,...  7.68 us
  transfers between devices with their start and end apart: 2, of which 2 were waited for; matrix products, arithmetic and copies ran while one was open for 2% of the time, Pallas kernels for 0%

profile of v1, /device:TPU:8, one launch (start us, length us, event | category | flops | bytes accessed | tf_op | source)
XLA Modules:
  0.0 133.1 jit_solution(11063811587741562076)
XLA Ops:
  0.6 0.0 copy-start
  0.6 1.0 convert.23
  1.6 0.1 bitcast_reduce_fusion
  1.8 0.3 multiply_reduce_fusion.2
  2.1 0.9 multiply_convert_fusion.1
  2.9 0.0 copy-done
  2.9 0.1 fusion.2
  3.1 0.1 copy.64
  3.2 0.1 broadcast_in_dim.7
  3.3 1.0 pad_maximum_fusion
  4.3 0.0 copy-start.1
  4.3 0.0 copy-start.2
  4.3 20.0 %all-to-all-start = ((bf16[128,20,128]{2,1,0:T(8,128)(2,1)}), bf16[128,20,128]{2,1,0:T(8,128)(2,1)S(1)}, u32[]{:S(2)}, u32[]{:S(2)}) async-start(bf16[128,20,128]{2,1,0:T(8,128)(2,1)} %pad_maximum_fusion), calls=%async_computation | async-start | bytes 1572864 | tf_op jit(solution)/shard_map/all_to_all | solution.py:118
  24.3 0.0 copy-done.1
  24.3 0.7 copy.29
  25.0 0.0 copy-done.2
  25.0 0.8 copy.30
  25.8 25.4 %all-to-all-done = bf16[128,20,128]{2,1,0:T(8,128)(2,1)S(1)} async-done(((bf16[128,20,128]{2,1,0:T(8,128)(2,1)}), bf16[128,20,128]{2,1,0:T(8,128)(2,1)S(1)}, u32[]{:S(2)}, u32[]{:S(2)}) %all-to-all-start) | async-done | bytes 655392 | tf_op jit(solution)/shard_map/all_to_all | solution.py:118
  51.2 1.0 copy.63
  52.2 7.7 %shard_map.101 = bf16[25,128,128]{2,1,0:T(8,128)(2,1)} custom-call(bf16[20,128,128]{2,1,0:T(8,128)(2,1)} %bitcast.72, bf16[2,256,128]{2,1,0:T(8,128)(2,1)} %bitcast.77, bf16[128,512]{1,0:T(8,128)(2,1)} %w_ref.1, bf16[512,128]{1,0:T(8,128)(2,1)} %bitcast.78, bf16[128,128]{1,0:T(8,128)(2,1)} %wout_ref.1), custom_call_target="tpu_custom_call" | custom-call | flops 900000000 | bytes 3000000 | tf_op jit(solution)/shard_map/pallas_call | solution.py:107
  59.8 1.7 %copy.31 = bf16[128,25,128]{2,1,0:T(8,128)(2,1)S(1)} copy(bf16[128,25,128]{2,0,1:T(8,128)(2,1)} %bitcast.71) | data formatting | bytes 1638400 | tf_op jit(solution)/shard_map/transpose | solution.py:135
  61.5 38.0 %all_to_all.15 = bf16[128,25,128]{2,1,0:T(8,128)(2,1)S(1)} all-to-all(bf16[128,25,128]{2,1,0:T(8,128)(2,1)S(1)} %copy.31), channel_id=1, replica_groups=mesh['crop'=4,'row_0'=8,'row_1'=2,'row_2'=8] {'row_0','row_1','row_2'}, dimensions={0} | all-to-all | bytes 1638400 | tf_op jit(solution)/shard_map/all_to_all | solution.py:118
  99.6 0.1 slice.43
  99.7 0.0 copy-start.3
  99.7 0.2 convert_reduce_fusion
  100.0 0.2 fusion.3
  100.2 0.2 copy-done.3
  100.4 0.6 multiply_reduce_fusion
  101.0 0.9 broadcast_in_dim.8
  101.9 6.6 %all-to-all-start.2 = ((bf16[128,10,128]{2,1,0:T(8,128)(2,1)}), bf16[128,10,128]{2,1,0:T(8,128)(2,1)S(1)}, u32[]{:S(2)}, u32[]{:S(2)}) async-start(bf16[128,10,128]{2,1,0:T(8,128)(2,1)} %broadcast_in_dim.8), calls=%async_computation.2 | async-start | bytes 1048576 | tf_op jit(solution)/shard_map/all_to_all | solution.py:118
  108.5 0.3 fusion.5
  108.9 0.8 copy.34
  109.7 20.1 %all-to-all-done.2 = bf16[128,10,128]{2,1,0:T(8,128)(2,1)S(1)} async-done(((bf16[128,10,128]{2,1,0:T(8,128)(2,1)}), bf16[128,10,128]{2,1,0:T(8,128)(2,1)S(1)}, u32[]{:S(2)}, u32[]{:S(2)}) %all-to-all-start.2) | async-done | bytes 327712 | tf_op jit(solution)/shard_map/all_to_all | solution.py:118
  129.8 0.4 copy.37
  130.1 0.1 convert_multiply_fusion
  130.2 0.2 slice_reduce_fusion
  130.4 0.5 slice_bitcast_fusion.2
  130.9 0.6 slice_bitcast_fusion.1
  131.5 0.8 copy.38
  132.3 0.7 copy.39
  (12 shorter events, 0.2 us)
Async XLA Ops:
  0.6 2.3 %copy-start = (bf16[128,4]{0,1:T(4,128)(2,1)S(1)}, bf16[128,4]{0,1:T(4,128)(2,1)}, u32[]{:S(2)}) copy-start(bf16[128,4]{0,1:T(4,128)(2,1)} %param.10) | copy-start | bytes 3076
  4.3 20.0 %copy-start.1 = (bf16[256,2,128]{2,1,0:T(2,128)(2,1)S(1)}, bf16[256,2,128]{2,1,0:T(2,128)(2,1)}, u32[]{:S(2)}) copy-start(bf16[256,2,128]{2,1,0:T(2,128)(2,1)} %param.7) | copy-start | bytes 393220
  4.3 20.7 %copy-start.2 = (bf16[128,512]{1,0:T(8,128)(2,1)S(1)}, bf16[128,512]{1,0:T(8,128)(2,1)}, u32[]{:S(2)}) copy-start(bf16[128,512]{1,0:T(8,128)(2,1)} %w_ref.1) | copy-start | bytes 393220
  4.3 46.8 %all-to-all-start = ((bf16[128,20,128]{2,1,0:T(8,128)(2,1)}), bf16[128,20,128]{2,1,0:T(8,128)(2,1)S(1)}, u32[]{:S(2)}, u32[]{:S(2)}) async-start(bf16[128,20,128]{2,1,0:T(8,128)(2,1)} %pad_maximum_fusion), calls=%async_computation | async-start | bytes 1572864 | tf_op jit(solution)/shard_map/all_to_all | solution.py:118
  99.7 0.7 copy-start.3
  101.9 27.9 %all-to-all-start.2 = ((bf16[128,10,128]{2,1,0:T(8,128)(2,1)}), bf16[128,10,128]{2,1,0:T(8,128)(2,1)S(1)}, u32[]{:S(2)}, u32[]{:S(2)}) async-start(bf16[128,10,128]{2,1,0:T(8,128)(2,1)} %broadcast_in_dim.8), calls=%async_computation.2 | async-start | bytes 1048576 | tf_op jit(solution)/shard_map/all_to_all | solution.py:118

commit v2 on v1

--- a/solution.py
+++ b/solution.py
@@ -114,8 +114,14 @@
     )(cols, grads, w, w_t, w_out)
 
 
-def exchanged(blocks):
-    return lax.all_to_all(blocks, ROW, split_axis=0, concat_axis=0, tiled=True)
+def exchanged(blocks, group):
+    rows = blocks.shape[1]
+    spare = -rows % group
+    if spare:
+        blocks = jnp.concatenate([blocks, jnp.zeros((DEV, spare, C), blocks.dtype)], axis=1)
+    blocks = blocks.reshape(DEV, -1, group, C)
+    moved = lax.all_to_all(blocks, ROW, split_axis=0, concat_axis=0, tiled=True)
+    return moved.reshape(DEV, -1, C)[:, :rows]
 
 
 def per_device(pair, out_grad, w_qkvg, w_out, w_bias, gain):
@@ -129,10 +135,10 @@
         ],
         axis=1,
     )
-    cols = exchanged(sent).transpose(1, 0, 2)
+    cols = exchanged(sent, 4).transpose(1, 0, 2)
     grads = out_grad.reshape(128, 2, 2, C).transpose(2, 1, 0, 3).reshape(2, N, C)
     planes = attention(cols, grads, w_qkvg, w_qkvg.T, w_out)
-    back = exchanged(planes.transpose(1, 0, 2))
+    back = exchanged(planes.transpose(1, 0, 2), 2)
     summed = jnp.sum(
         jnp.concatenate([back[:, :16], back[:, 20:]], axis=1).astype(F32), axis=0
     )
@@ -157,7 +163,7 @@
     ).astype(BF16)
     d_pair = d_pair.transpose(0, 2, 1, 3).reshape(2, N, C)
     own = jnp.concatenate([summed[16:], d_wbias, d_gain[None]], axis=0).astype(BF16)
-    last = exchanged(jnp.broadcast_to(own[None], (DEV, 10, C))).astype(F32) * (1.0 / N)
+    last = exchanged(jnp.broadcast_to(own[None], (DEV, 10, C)), 2).astype(F32) * (1.0 / N)
     small = jnp.sum(last[:, 5:], axis=0)
     return (
         d_pair,

time: 133 us -> 122 us (0.917)
  waiting for transfers between devices: 45.5 us -> 39.5 us
  blocking collectives: 38 us -> 33.7 us
  other arithmetic: 4.12 us -> 2.24 us
    all_to_all x2, waiting for transfers between devices: 45.5 us -> 39.5 us  [exchanged(): moved = lax.all_to_all(blocks, ROW, split_axis=0, concat_axis=0, tiled=True)]
    all_to_all x1, blocking collectives: 38 us -> 33.7 us  [exchanged(): moved = lax.all_to_all(blocks, ROW, split_axis=0, concat_axis=0, tiled=True)]
    reshape x1 -> x2, local copies, waits for them, and re-layouts: 0.12 us -> 2.22 us  [exchanged(): blocks = blocks.reshape(DEV, -1, group, C)]
    transpose x1 -> x0, local copies, waits for them, and re-layouts: 1.7 us -> none  [per_device(): back = exchanged(planes.transpose(1, 0, 2))]
where the time goes in v2:
time: 122 us
  waiting for transfers between devices  39.5 us (32%)
  blocking collectives  33.7 us (28%)
  starting transfers between devices  26.7 us (22%)
  local copies, waits for them, and re-layouts  10.6 us (9%)
  Pallas kernels  7.68 us (6%)
  other arithmetic  2.24 us (2%)
    all_to_all x2, waiting for transfers between devices, exchanged(): moved = lax.all_to_all(blocks, ROW, split_axis=0, concat_axis=0, tiled=True)  39.5 us
    all_to_all x1, blocking collectives, exchanged(): moved = lax.all_to_all(blocks, ROW, split_axis=0, concat_axis=0, tiled=True)  33.7 us
    all_to_all x2, starting transfers between devices, exchanged(): moved = lax.all_to_all(blocks, ROW, split_axis=0, concat_axis=0, tiled=True)  26.7 us
    pallas_call x1, Pallas kernels, attention(): pl.pallas_call(attention_kernel, out_shape=jax.ShapeDtypeStruct((25, DEV,...  7.68 us
  transfers between devices with their start and end apart: 2, of which 2 were waited for; matrix products, arithmetic and copies ran while one was open for 2% of the time, Pallas kernels for 0%

profile of v2, /device:TPU:8, one launch (start us, length us, event | category | flops | bytes accessed | tf_op | source)
XLA Modules:
  0.0 122.1 jit_solution(4364157423507681528)
XLA Ops:
  0.6 0.0 copy-start
  0.6 0.0 copy-start.3
  0.7 1.0 convert.29
  1.7 0.1 bitcast_reduce_fusion
  1.8 0.3 multiply_reduce_fusion.2
  2.1 0.0 copy-done.3
  2.1 0.2 multiply_convert_fusion.1
  2.3 0.0 copy-done
  2.3 0.1 fusion.2
  2.5 0.1 broadcast_in_dim.7
  2.5 0.1 pad_maximum_fusion
  2.6 1.3 %copy.57 = bf16[128,5,4,128]{3,2,1,0:T(4,128)(2,1)} copy(bf16[128,5,4,128]{3,0,2,1:T(8,128)(2,1)S(1)} %bitcast.81) | data formatting | bytes 1310720 | tf_op jit(solution)/shard_map/reshape | solution.py:122
  4.0 0.0 copy-start.1
  4.0 0.0 copy-start.2
  4.0 20.0 %all-to-all-start = ((bf16[128,5,4,128]{3,2,1,0:T(4,128)(2,1)}), bf16[128,5,4,128]{3,2,1,0:T(4,128)(2,1)S(1)}, u32[]{:S(2)}, u32[]{:S(2)}) async-start(bf16[128,5,4,128]{3,2,1,0:T(4,128)(2,1)} %copy.57), calls=%async_computation | async-start | bytes 1310720 | tf_op jit(solution)/shard_map/all_to_all | solution.py:123
  23.9 0.0 copy-done.1
  23.9 0.7 copy.59
  24.6 0.0 copy-done.2
  24.6 0.8 copy.60
  25.4 23.0 %all-to-all-done = bf16[128,5,4,128]{3,2,1,0:T(4,128)(2,1)S(1)} async-done(((bf16[128,5,4,128]{3,2,1,0:T(4,128)(2,1)}), bf16[128,5,4,128]{3,2,1,0:T(4,128)(2,1)S(1)}, u32[]{:S(2)}, u32[]{:S(2)}) %all-to-all-start) | async-done | bytes 655392 | tf_op jit(solution)/shard_map/all_to_all | solution.py:123
  48.4 1.0 copy.58
  49.3 7.7 %shard_map.101 = bf16[25,128,128]{2,1,0:T(8,128)(2,1)} custom-call(bf16[20,128,128]{2,1,0:T(8,128)(2,1)} %bitcast.89, bf16[2,256,128]{2,1,0:T(8,128)(2,1)} %bitcast.93, bf16[128,512]{1,0:T(8,128)(2,1)} %w_ref.1, bf16[512,128]{1,0:T(8,128)(2,1)} %bitcast.94, bf16[128,128]{1,0:T(8,128)(2,1)} %wout_ref.1), custom_call_target="tpu_custom_call" | custom-call | flops 900000000 | bytes 3000000 | tf_op jit(solution)/shard_map/pallas_call | solution.py:107
  57.0 1.2 concatenate.23
  58.3 0.9 copy.61
  59.1 33.7 %all_to_all.15 = bf16[128,13,2,128]{3,2,1,0:T(2,128)(2,1)S(1)} all-to-all(bf16[128,13,2,128]{3,2,1,0:T(2,128)(2,1)S(1)} %copy.61), channel_id=1, replica_groups=mesh['crop'=4,'row_0'=8,'row_1'=2,'row_2'=8] {'row_0','row_1','row_2'}, dimensions={0} | all-to-all | bytes 1703936 | tf_op jit(solution)/shard_map/all_to_all | solution.py:123
  92.8 0.2 copy.62
  93.1 0.1 convert_reduce_fusion
  93.2 0.2 fusion.4
  93.4 0.6 multiply_reduce_fusion
  94.0 0.9 broadcast_in_dim.8
  94.9 6.7 %all-to-all-start.2 = ((bf16[128,5,2,128]{3,2,1,0:T(2,128)(2,1)}), bf16[128,5,2,128]{3,2,1,0:T(2,128)(2,1)S(1)}, u32[]{:S(2)}, u32[]{:S(2)}) async-start(bf16[128,5,2,128]{3,2,1,0:T(2,128)(2,1)} %broadcast_in_dim.8), calls=%async_computation.2 | async-start | bytes 655360 | tf_op jit(solution)/shard_map/all_to_all | solution.py:123
  101.6 0.3 fusion.6
  102.0 0.8 copy.64
  102.8 16.5 %all-to-all-done.2 = bf16[128,5,2,128]{3,2,1,0:T(2,128)(2,1)S(1)} async-done(((bf16[128,5,2,128]{3,2,1,0:T(2,128)(2,1)}), bf16[128,5,2,128]{3,2,1,0:T(2,128)(2,1)S(1)}, u32[]{:S(2)}, u32[]{:S(2)}) %all-to-all-start.2) | async-done | bytes 327712 | tf_op jit(solution)/shard_map/all_to_all | solution.py:123
  119.3 0.6 slice_bitcast_fusion
  120.0 0.6 slice_bitcast_fusion.1
  120.6 0.5 slice_bitcast_fusion.2
  121.1 0.1 copy.72
  121.2 0.8 copy.69
  (14 shorter events, 0.2 us)
Async XLA Ops:
  0.6 1.7 %copy-start = (bf16[128,4]{0,1:T(4,128)(2,1)S(1)}, bf16[128,4]{0,1:T(4,128)(2,1)}, u32[]{:S(2)}) copy-start(bf16[128,4]{0,1:T(4,128)(2,1)} %param.10) | copy-start | bytes 3076
  0.6 1.4 %copy-start.3 = (f32[128]{0:T(128)S(1)}, f32[128]{0:T(128)}, u32[]{:S(2)}) copy-start(f32[128]{0:T(128)} %param.11) | copy-start | bytes 1540
  4.0 20.0 %copy-start.1 = (bf16[256,2,128]{2,1,0:T(2,128)(2,1)S(1)}, bf16[256,2,128]{2,1,0:T(2,128)(2,1)}, u32[]{:S(2)}) copy-start(bf16[256,2,128]{2,1,0:T(2,128)(2,1)} %param.7) | copy-start | bytes 393220
  4.0 20.7 %copy-start.2 = (bf16[128,512]{1,0:T(8,128)(2,1)S(1)}, bf16[128,512]{1,0:T(8,128)(2,1)}, u32[]{:S(2)}) copy-start(bf16[128,512]{1,0:T(8,128)(2,1)} %w_ref.1) | copy-start | bytes 393220
  4.0 44.4 %all-to-all-start = ((bf16[128,5,4,128]{3,2,1,0:T(4,128)(2,1)}), bf16[128,5,4,128]{3,2,1,0:T(4,128)(2,1)S(1)}, u32[]{:S(2)}, u32[]{:S(2)}) async-start(bf16[128,5,4,128]{3,2,1,0:T(4,128)(2,1)} %copy.57), calls=%async_computation | async-start | bytes 1310720 | tf_op jit(solution)/shard_map/all_to_all | solution.py:123
  94.9 24.3 %all-to-all-start.2 = ((bf16[128,5,2,128]{3,2,1,0:T(2,128)(2,1)}), bf16[128,5,2,128]{3,2,1,0:T(2,128)(2,1)S(1)}, u32[]{:S(2)}, u32[]{:S(2)}) async-start(bf16[128,5,2,128]{3,2,1,0:T(2,128)(2,1)} %broadcast_in_dim.8), calls=%async_computation.2 | async-start | bytes 655360 | tf_op jit(solution)/shard_map/all_to_all | solution.py:123
